TPU v7x, 256 devices: a whole 4x4x8 slice. The times are simulated.
256 devices in a mesh: seq: 64 (over x, z, core), head: 4 (over y).
Axes of the slice: x: 4, y: 4, z: 8, core: 2. Of those that a mesh axis runs over, the one named last changes fastest.
Arguments:
- tokens: bfloat16 [21504, 4096], P('seq', 'head')
- w_short: float32 [3, 4096], P(None, 'head'), may hold values from 0.25 to 1.5
- w_query: bfloat16 [4096, 2048], P(None, 'head')
- w_key: bfloat16 [4096, 2048], P(None, 'head')
- w_value: bfloat16 [4096, 2048], P(None, 'head'), may hold values from -0.09375 to 0.09375
- owner_lengths: int32 [64], replicated, may hold values from 1 to 224, as said below
Outputs:
- attended: bfloat16 [14336, 2048], P('seq', 'head')
Inputs may be any that keep to these rules, and one draw needn't show every extreme that they name: The counts sum to 7168; owner o holds the coarse rows from starts[o] on, with o * 112 <= starts[o] and starts[o] + owner_lengths[o] <= (o + 2) * 112; the largest count is exactly 224.
All inputs are finite; a program needn't handle non-finite values.
Results may differ from a plain program's by a relative error of at most 0.012.
The roundings to bfloat16 on the way count: a program that leaves them out, or rounds other values in their place, can miss the bound.
Values may be sent and summed in bfloat16 or wider, within the bound.
A program may use at most 128 MiB of HBM per device.

v0:
```python
import math
import jax
import jax.numpy as jnp
from jax import lax
from jax.sharding import PartitionSpec as P

HD = 128
masked_score = -1e30


def from_behind(x, axis, by):
    devices = lax.axis_size(axis)
    pairs = [(i, i + by) for i in range(devices) if 0 <= i + by < devices]
    return lax.ppermute(x, axis, pairs)


def block_scores(owned, key_block, offset, query_pos):
    length = key_block.shape[0]
    keyed = key_block.reshape(length, owned.shape[1], HD)
    scores = jnp.einsum("qhd,khd->hqk", owned, keyed, preferred_element_type=jnp.float32) * (
        1.0 / math.sqrt(HD)
    )
    key_pos = offset + jnp.arange(length, dtype=jnp.int32)
    allowed = key_pos[None, :] <= query_pos[:, None]
    return jnp.where(allowed[None], scores, masked_score)


def block_context(owned, key_block, value_block, offset, query_pos, maxima):
    scores = block_scores(owned, key_block, offset, query_pos)
    weights = jnp.exp(scores - maxima[:, :, None])
    length = value_block.shape[0]
    valued = value_block.reshape(length, owned.shape[1], HD)
    added = jnp.einsum(
        "hqk,khd->hqd", weights.astype(jnp.bfloat16), valued, preferred_element_type=jnp.float32
    )
    return (jnp.sum(weights, axis=2), added)


def shards(tokens, w_short, w_query, w_key, w_value, owner_lengths):
    rows_local = tokens.shape[0]
    coarse_local = rows_local // 3
    width_part = tokens.shape[1]
    seq_count = lax.axis_size("seq")
    position = lax.axis_index("seq")
    boundary = from_behind(tokens[rows_local - 2 :], "seq", 1)
    shifted = jnp.concatenate([boundary, tokens[: rows_local - 2]], axis=0)
    grouped = shifted.reshape(coarse_local, 3, width_part)
    pooled = (
        grouped[:, 0].astype(jnp.float32) * w_short[0]
        + grouped[:, 1].astype(jnp.float32) * w_short[1]
        + grouped[:, 2].astype(jnp.float32) * w_short[2]
    )
    squares = lax.psum(jnp.sum(pooled * pooled, axis=1), "head")
    full_width = width_part * lax.axis_size("head")
    norm_scale = lax.rsqrt(squares / full_width + 1e-05)
    coarse_part = (pooled * norm_scale[:, None]).astype(jnp.bfloat16)
    features = w_query.shape[1]
    zero_sums = jnp.zeros((coarse_local, features), jnp.float32)
    carried = (zero_sums, zero_sums, zero_sums)
    shard_rows = lax.all_gather(coarse_part, "head", axis=1, tiled=True)
    outputs = []
    for running, weight in zip(carried, (w_query, w_key, w_value)):
        outputs.append(jnp.dot(shard_rows, weight, preferred_element_type=jnp.float32))
    query_sum, key_sum, value_sum = tuple(outputs)
    queries = query_sum.astype(jnp.bfloat16)
    key_rows = key_sum.astype(jnp.bfloat16)
    value_rows = value_sum.astype(jnp.bfloat16)
    starts = jnp.cumsum(owner_lengths) - owner_lengths
    owners = jnp.arange(seq_count, dtype=jnp.int32)
    chosen = owners == position
    first_row = jnp.sum(jnp.where(chosen, starts, 0))
    row_count = jnp.sum(jnp.where(chosen, owner_lengths, 0))
    capacity = 2 * coarse_local
    following = from_behind(queries, "seq", -1)
    window = jnp.concatenate(
        [queries, following, jnp.zeros((coarse_local, features), jnp.bfloat16)], axis=0
    )
    local_start = first_row - position * coarse_local
    owned_rows = lax.dynamic_slice_in_dim(window, local_start, capacity, 0)
    head_count = features // HD
    owned = owned_rows.reshape(capacity, head_count, HD)
    query_pos = first_row + jnp.arange(capacity, dtype=jnp.int32)
    last_row = first_row + row_count
    coarse_total = seq_count * coarse_local
    start_max = jnp.full((head_count, capacity), masked_score, jnp.float32)
    start_sums = (
        jnp.zeros((head_count, capacity), jnp.float32),
        jnp.zeros((head_count, capacity, HD), jnp.float32),
    )
    key_all, value_all = (
        lax.all_gather(key_rows, "seq", axis=0, tiled=True),
        lax.all_gather(value_rows, "seq", axis=0, tiled=True),
    )
    block_size = math.gcd(coarse_total, 512)
    blocks = (last_row + block_size - 1) // block_size

    def find_max(index, maxima):
        key_block = lax.dynamic_slice_in_dim(key_all, index * block_size, block_size, 0)
        return jnp.maximum(
            maxima, jnp.max(block_scores(owned, key_block, index * block_size, query_pos), axis=2)
        )

    maxima = lax.fori_loop(0, blocks, find_max, start_max)

    def add_block(index, carried):
        offset = index * block_size
        key_block = lax.dynamic_slice_in_dim(key_all, offset, block_size, 0)
        value_block = lax.dynamic_slice_in_dim(value_all, offset, block_size, 0)
        sums, added = block_context(owned, key_block, value_block, offset, query_pos, maxima)
        return (carried[0] + sums, carried[1] + added)

    totals, context = lax.fori_loop(0, blocks, add_block, start_sums)
    result = (context / totals[:, :, None]).transpose(1, 0, 2).reshape(capacity, features)
    live = jnp.arange(capacity, dtype=jnp.int32) < row_count
    return jnp.where(live[:, None], result, 0.0).astype(jnp.bfloat16)


def solution(mesh):
    return jax.shard_map(
        shards,
        mesh=mesh,
        in_specs=(
            P("seq", "head"),
            P(None, "head"),
            P(None, "head"),
            P(None, "head"),
            P(None, "head"),
            P(),
        ),
        out_specs=P("seq", "head"),
        check_vma=False,
    )
```

profile of v0, /device:TPU:199, one launch (start us, length us, event | category | flops | bytes accessed | tf_op | source)
XLA Modules:
  0.0 273.7 jit_solution(7263793353940745998)
XLA Ops:
  7.3 3.2 %collective-permute-start = (bf16[2,1024]{1,0:T(2,128)(2,1)S(1)}, bf16[2,1024]{1,0:T(2,128)(2,1)S(1)}, u32[]{:S(2)}, u32[]{:S(2)}) collective-permute-start(bf16[2,1024]{1,0:T(2,128)(2,1)S(1)} %slice.24), channel_id=1, source_target_pairs={{0,4},{4,8},{8,12},{12,16},{16,20},{20,24},{24,28},{28,32},{32,36}... | collective-permute-start | bytes 12296 | tf_op jit(solution)/shard_map/ppermute | solution.py:14
  10.5 0.8 fusion.19
  11.3 1.3 pad_maximum_fusion
  13.1 0.9 fusion.18
  14.4 8.7 %psum.7 = f32[112]{0:T(128)S(1)} all-reduce(f32[112]{0:T(128)S(1)} %get-tuple-element.175), channel_id=1, replica_groups=mesh['seq'=64,'head'=4] {'head'}, use_global_device_ids=true, to_apply=%region_4.5 | all-reduce | flops 112 | bytes 896 | tf_op jit(solution)/shard_map/psum | solution.py:53
  23.3 12.6 %all_gather.9 = bf16[112,4096]{1,0:T(8,128)(2,1)S(1)} all-gather(bf16[112,1024]{1,0:T(8,128)(2,1)S(1)} %multiply_convert_fusion), channel_id=1, replica_groups=mesh['seq'=64,'head'=4] {'head'}, dimensions={1}, use_global_device_ids=true | all-gather | bytes 1146880 | tf_op jit(solution)/shard_map/all_gather | solution.py:60
  35.9 3.6 %convolution_convert_fusion.2 = bf16[112,512]{1,0:T(8,128)(2,1)} fusion(bf16[112,4096]{1,0:T(8,128)(2,1)S(1)} %all_gather.9, bf16[4096,512]{1,0:T(8,128)(2,1)} %param.13), kind=kOutput, calls=%fused_computation.20 | convolution fusion | flops 469819392 | bytes 5226496 | tf_op jit(solution)/shard_map/dot_general | solution.py:63
  39.6 3.6 %convolution_convert_fusion = bf16[112,512]{1,0:T(8,128)(2,1)} fusion(bf16[112,4096]{1,0:T(8,128)(2,1)S(1)} %all_gather.9, bf16[4096,512]{1,0:T(8,128)(2,1)} %param.14), kind=kOutput, calls=%fused_computation.18 | convolution fusion | flops 469819392 | bytes 5226496 | tf_op jit(solution)/shard_map/dot_general | solution.py:63
  44.2 2.9 %convolution_convert_fusion.1 = bf16[112,512]{1,0:T(8,128)(2,1)S(1)} fusion(bf16[112,4096]{1,0:T(8,128)(2,1)S(1)} %all_gather.9, bf16[4096,512]{1,0:T(8,128)(2,1)} %param.12), kind=kOutput, calls=%fused_computation.19 | convolution fusion | flops 469819392 | bytes 5226496 | tf_op jit(solution)/shard_map/dot_general | solution.py:63
  47.2 6.4 %collective-permute-start.1 = (bf16[112,512]{1,0:T(8,128)(2,1)S(1)}, bf16[112,512]{1,0:T(8,128)(2,1)S(1)}, u32[]{:S(2)}, u32[]{:S(2)}) collective-permute-start(bf16[112,512]{1,0:T(8,128)(2,1)S(1)} %convolution_convert_fusion.1), channel_id=1, source_target_pairs={{4,0},{8,4},{12,8},{16,12},{20,16},{24,20},{28,24},{32,28},{36,32}... | collective-permute-start | bytes 344072 | tf_op jit(solution)/shard_map/ppermute | solution.py:14
  56.3 1.3 collective-permute-done.1
  57.8 65.8 %all-gather.3.cloned.1.call-done = bf16[7168,512]{1,0:T(8,128)(2,1)} async-done(((bf16[112,512]{1,0:T(8,128)(2,1)}), bf16[7168,512]{1,0:T(8,128)(2,1)}) %all-gather.3.cloned.1.call-update) | async-done | bytes 7340048 | tf_op jit(solution)/shard_map/all_gather | solution.py:91
  123.5 10.1 %copy.19 = bf16[7168,512]{0,1:T(8,128)(2,1)} copy(bf16[7168,512]{1,0:T(8,128)(2,1)} %all-gather.3.cloned.1.call-done) | data formatting | bytes 14680064
  133.6 33.0 %while.24 = (s32[]{:T(128)}, f32[4,224]{1,0:T(4,128)S(1)}, s32[]{:T(128)}, bf16[7168,512]{0,1:T(8,128)(2,1)}, bf16[224,4,128]{2,0,1:T(8,128)(2,1)S(1)}, /*index=...) while((s32[]{:T(128)}, f32[4,224]{1,0:T(4,128)S(1)}, s32[]{:T(128)}, ...), condition=%wide.region_7.8_spmd.clone, body=%wide.region_5.7_spmd.clone.sunk | while | flops 118932200 | bytes 2052007 | solution.py:103
  133.6 1.1 constant_dynamic-slice_fusion.6
  135.9 1.1 constant_dynamic-slice_fusion.6
  138.3 1.1 constant_dynamic-slice_fusion.6
  140.7 1.1 constant_dynamic-slice_fusion.6
  143.0 1.1 constant_dynamic-slice_fusion.6
  145.4 1.1 constant_dynamic-slice_fusion.6
  147.7 1.1 constant_dynamic-slice_fusion.6
  150.1 1.1 constant_dynamic-slice_fusion.6
  152.5 1.1 constant_dynamic-slice_fusion.6
  154.8 1.1 constant_dynamic-slice_fusion.6
  157.2 1.1 constant_dynamic-slice_fusion.6
  159.5 1.1 constant_dynamic-slice_fusion.6
  161.9 1.1 constant_dynamic-slice_fusion.6
  164.3 1.1 constant_dynamic-slice_fusion.6
  166.6 38.5 %all-gather.5.cloned.1.call-done = bf16[7168,512]{1,0:T(8,128)(2,1)} async-done(((bf16[112,512]{1,0:T(8,128)(2,1)}), bf16[7168,512]{1,0:T(8,128)(2,1)}) %all-gather.5.cloned.1.call-update) | async-done | bytes 7340048 | tf_op jit(solution)/shard_map/all_gather | solution.py:92
  205.2 60.7 %while.25 = (s32[]{:T(128)}, f32[4,224]{1,0:T(4,128)S(1)}, f32[4,224,128]{2,1,0:T(8,128)S(1)}, s32[]{:T(128)}, bf16[7168,512]{0,1:T(8,128)(2,1)}, /*index=5*/bf1...) while((s32[]{:T(128)}, f32[4,224]{1,0:T(4,128)S(1)}, ...), condition=%wide.region_10.11_spmd.clone, body=%wide.region_8.10_spmd.clone.sunk | while | flops 237404896 | bytes 7429571 | solution.py:112
  205.2 1.1 constant_dynamic-slice_fusion.7
  207.0 0.8 fusion.48
  207.8 1.1 constant_dynamic-slice_fusion.8
  209.5 1.1 constant_dynamic-slice_fusion.7
  211.4 0.8 fusion.48
  212.1 1.1 constant_dynamic-slice_fusion.8
  213.9 1.1 constant_dynamic-slice_fusion.7
  216.5 1.1 constant_dynamic-slice_fusion.8
  218.2 1.1 constant_dynamic-slice_fusion.7
  220.8 1.1 constant_dynamic-slice_fusion.8
  222.5 1.1 constant_dynamic-slice_fusion.7
  225.1 1.1 constant_dynamic-slice_fusion.8
  226.9 1.1 constant_dynamic-slice_fusion.7
  228.7 0.8 fusion.48
  229.5 1.1 constant_dynamic-slice_fusion.8
  231.2 1.1 constant_dynamic-slice_fusion.7
  233.0 0.8 fusion.48
  233.8 1.1 constant_dynamic-slice_fusion.8
  235.6 1.1 constant_dynamic-slice_fusion.7
  237.4 0.8 fusion.48
  238.1 1.1 constant_dynamic-slice_fusion.8
  239.9 1.1 constant_dynamic-slice_fusion.7
  242.5 1.1 constant_dynamic-slice_fusion.8
  244.2 1.1 constant_dynamic-slice_fusion.7
  246.8 1.1 constant_dynamic-slice_fusion.8
  248.6 1.1 constant_dynamic-slice_fusion.7
  251.1 1.1 constant_dynamic-slice_fusion.8
  252.9 1.1 constant_dynamic-slice_fusion.7
  255.5 1.1 constant_dynamic-slice_fusion.8
  257.2 1.1 constant_dynamic-slice_fusion.7
  259.8 1.1 constant_dynamic-slice_fusion.8
  261.6 1.1 constant_dynamic-slice_fusion.7
  264.2 1.1 constant_dynamic-slice_fusion.8
  265.9 0.9 fusion.8
  (186 shorter events, 46.9 us)
Async XLA Ops:
  6.5 117.0 %all-gather.3.cloned.1.call-start = ((), (), s32[]{:S(2)}) async-start(), calls=%async_computation | async-start | bytes 7454720 | tf_op jit(solution)/shard_map/all_gather | solution.py:91
  7.3 4.1 %collective-permute-start = (bf16[2,1024]{1,0:T(2,128)(2,1)S(1)}, bf16[2,1024]{1,0:T(2,128)(2,1)S(1)}, u32[]{:S(2)}, u32[]{:S(2)}) collective-permute-start(bf16[2,1024]{1,0:T(2,128)(2,1)S(1)} %slice.24), channel_id=1, source_target_pairs={{0,4},{4,8},{8,12},{12,16},{16,20},{20,24},{24,28},{28,32},{32,36}... | collective-permute-start | bytes 12296 | tf_op jit(solution)/shard_map/ppermute | solution.py:14
  35.9 7.3 %copy-start = (s32[64]{0:T(128)S(1)}, s32[64]{0:T(128)}, u32[]{:S(2)}) copy-start(s32[64]{0:T(128)} %param.15) | copy-start | bytes 772
  39.5 165.6 %all-gather.5.cloned.1.call-start = ((), (), s32[]{:S(2)}) async-start(), calls=%async_computation.1 | async-start | bytes 7454720 | tf_op jit(solution)/shard_map/all_gather | solution.py:92
  47.2 10.4 %collective-permute-start.1 = (bf16[112,512]{1,0:T(8,128)(2,1)S(1)}, bf16[112,512]{1,0:T(8,128)(2,1)S(1)}, u32[]{:S(2)}, u32[]{:S(2)}) collective-permute-start(bf16[112,512]{1,0:T(8,128)(2,1)S(1)} %convolution_convert_fusion.1), channel_id=1, source_target_pairs={{4,0},{8,4},{12,8},{16,12},{20,16},{24,20},{28,24},{32,28},{36,32}... | collective-permute-start | bytes 344072 | tf_op jit(solution)/shard_map/ppermute | solution.py:14
Sparse Core Ops, SparseCore 0:
  39.6 83.8 all-gather.2
  126.3 78.8 all-gather.4
where the time goes:
time: 277 us; the launch traced here: 274 us
  waiting for transfers between devices  106 us (38%)
  local copies, waits for them, and re-layouts  60.7 us (22%)
  matrix products  33.8 us (12%)
  other arithmetic  25.7 us (9%)
  blocking collectives  21.3 us (8%)
  between operations  15.4 us (6%)
  starting transfers between devices  9.67 us (3%)
    all_gather x1, waiting for transfers between devices, shards(): lax.all_gather(key_rows, 'seq', axis=0, tiled=True)  65.8 us
    all_gather x1, waiting for transfers between devices, shards(): lax.all_gather(value_rows, 'seq', axis=0, tiled=True)  38.5 us
    dynamic_slice x28, local copies, waits for them, and re-layouts, add_block(): value_block = lax.dynamic_slice_in_dim(value_all, offset, block_size, 0)  18.1 us
    dot_general x28, matrix products, block_scores(): jnp.einsum('qhd,khd->hqk', owned, keyed, preferred_element_type=jnp.float32)  17.6 us
    add x28, other arithmetic, shards(): query_pos = first_row + jnp.arange(capacity, dtype=jnp.int32)  16.1 us
    dynamic_slice x14, local copies, waits for them, and re-layouts, find_max(): lax.dynamic_slice_in_dim(key_all, index * block_size, block_size, 0)  15.2 us
    dynamic_slice x14, local copies, waits for them, and re-layouts, add_block(): key_block = lax.dynamic_slice_in_dim(key_all, offset, block_size, 0)  15.1 us
    all_gather x1, blocking collectives, shards(): shard_rows = lax.all_gather(coarse_part, 'head', axis=1, tiled=True)  12.6 us
  transfers between devices with their start and end apart: 4, of which 3 were waited for; matrix products, arithmetic and copies ran while one was open for 19% of the time, Pallas kernels for 0%

commit v1 on v0

--- a/solution.py
+++ b/solution.py
@@ -88,7 +88,9 @@
         jnp.zeros((head_count, capacity, HD), jnp.float32),
     )
     key_all, value_all = (
-        lax.all_gather(key_rows, "seq", axis=0, tiled=True),
+        jnp.concatenate(
+            lax.all_to_all(jnp.stack([key_rows] * lax.axis_size("seq")), "seq", 0, 0), axis=0
+        ),
         lax.all_gather(value_rows, "seq", axis=0, tiled=True),
     )
     block_size = math.gcd(coarse_total, 512)

time: 277 us -> 357 us (1.29)
  waiting for transfers between devices: 106 us -> 169 us
  starting transfers between devices: 9.67 us -> 21.5 us
  local copies, waits for them, and re-layouts: 60.7 us -> 64.6 us
    ppermute x2, waiting for transfers between devices: 1.29 us -> 169 us  [from_behind(): return lax.ppermute(x, axis, pairs)]
    all_gather x1 -> x0, waiting for transfers between devices: 65.8 us -> none  [shards(): lax.all_gather(key_rows, 'seq', axis=0, tiled=True)]
    all_gather x1, waiting for transfers between devices: 38.5 us -> 0.02 us  [shards(): lax.all_gather(value_rows, 'seq', axis=0, tiled=True)]
    all_to_all x0 -> x1, starting transfers between devices: none -> 16 us  [shards(): lax.all_to_all(jnp.stack([key_rows] * lax.axis_size('seq')), 'seq', 0, 0)]
    ppermute x2, starting transfers between devices: 9.63 us -> 5.45 us  [from_behind(): return lax.ppermute(x, axis, pairs)]
    another operation x1 -> x2, local copies, waits for them, and re-layouts: 0.1 us -> 4.01 us  [the longest x1 3.91 us: shards(): jnp.stack([key_rows] * lax.axis_size('seq'))]
  transfers between devices with their start and end apart: 4 -> 4, of which waited for: 3 -> 1; matrix products, arithmetic and copies ran while one was open for 19% -> 15% of each run, Pallas kernels for 0% -> 0%
where the time goes in v1:
time: 357 us; the launch traced here: 354 us
  waiting for transfers between devices  169 us (47%)
  local copies, waits for them, and re-layouts  64.6 us (18%)
  matrix products  33.1 us (9%)
  other arithmetic  27.4 us (8%)
  starting transfers between devices  21.5 us (6%)
  blocking collectives  21.3 us (6%)
  between operations  15.5 us (4%)
    ppermute x2, waiting for transfers between devices, from_behind(): return lax.ppermute(x, axis, pairs)  169 us
    dynamic_slice x28, local copies, waits for them, and re-layouts, add_block(): value_block = lax.dynamic_slice_in_dim(value_all, offset, block_size, 0)  18.1 us
    add x28, other arithmetic, shards(): query_pos = first_row + jnp.arange(capacity, dtype=jnp.int32)  17.9 us
    dot_general x28, matrix products, block_scores(): jnp.einsum('qhd,khd->hqk', owned, keyed, preferred_element_type=jnp.float32)  17.6 us
    all_to_all x1, starting transfers between devices, shards(): lax.all_to_all(jnp.stack([key_rows] * lax.axis_size('seq')), 'seq', 0, 0)  16 us
    dynamic_slice x14, local copies, waits for them, and re-layouts, add_block(): key_block = lax.dynamic_slice_in_dim(key_all, offset, block_size, 0)  15.1 us
    dynamic_slice x14, local copies, waits for them, and re-layouts, find_max(): lax.dynamic_slice_in_dim(key_all, index * block_size, block_size, 0)  15.1 us
    all_gather x1, blocking collectives, shards(): shard_rows = lax.all_gather(coarse_part, 'head', axis=1, tiled=True)  12.6 us
  transfers between devices with their start and end apart: 4, of which 1 were waited for; matrix products, arithmetic and copies ran while one was open for 15% of the time, Pallas kernels for 0%

profile of v1, /device:TPU:199, one launch (start us, length us, event | category | flops | bytes accessed | tf_op | source)
XLA Modules:
  0.0 353.7 jit_solution(13786191954985210566)
XLA Ops:
  7.3 3.2 collective-permute-start
  10.5 0.8 fusion.19
  11.3 1.3 pad_maximum_fusion
  13.1 0.9 fusion.18
  14.4 8.7 %psum.7 = f32[112]{0:T(128)S(1)} all-reduce(f32[112]{0:T(128)S(1)} %get-tuple-element.190), channel_id=1, replica_groups=mesh['seq'=64,'head'=4] {'head'}, use_global_device_ids=true, to_apply=%region_4.5 | all-reduce | flops 112 | bytes 896 | tf_op jit(solution)/shard_map/psum | solution.py:53
  23.3 12.6 %all_gather.6 = bf16[112,4096]{1,0:T(8,128)(2,1)S(1)} all-gather(bf16[112,1024]{1,0:T(8,128)(2,1)S(1)} %multiply_convert_fusion), channel_id=1, replica_groups=mesh['seq'=64,'head'=4] {'head'}, dimensions={1}, use_global_device_ids=true | all-gather | bytes 1146880 | tf_op jit(solution)/shard_map/all_gather | solution.py:60
  35.9 2.9 convolution_convert_fusion.2
  38.8 3.9 %stack.2 = bf16[64,112,512]{2,1,0:T(8,128)(2,1)} broadcast(bf16[112,512]{1,0:T(8,128)(2,1)S(1)} %convolution_convert_fusion.2), dimensions={1,2} | broadcast | bytes 7454720 | tf_op jit(solution)/shard_map/stack | solution.py:92
  42.7 16.0 %all-to-all-start = ((bf16[64,112,512]{2,1,0:T(8,128)(2,1)}), bf16[64,112,512]{2,1,0:T(8,128)(2,1)}, u32[]{:S(2)}, u32[]{:S(2)}) async-start(bf16[64,112,512]{2,1,0:T(8,128)(2,1)} %stack.2), calls=%async_computation | async-start | bytes 14680064 | tf_op jit(solution)/shard_map/all_to_all | solution.py:92
  58.8 3.6 %convolution_convert_fusion = bf16[112,512]{1,0:T(8,128)(2,1)} fusion(bf16[112,4096]{1,0:T(8,128)(2,1)S(1)} %all_gather.6, bf16[4096,512]{1,0:T(8,128)(2,1)} %param.14), kind=kOutput, calls=%fused_computation.18 | convolution fusion | flops 469819392 | bytes 5226496 | tf_op jit(solution)/shard_map/dot_general | solution.py:63
  63.4 2.9 convolution_convert_fusion.1
  66.4 2.3 collective-permute-start.1
  71.3 168.7 %collective-permute-done.1 = bf16[112,512]{1,0:T(8,128)(2,1)S(1)} collective-permute-done((bf16[112,512]{1,0:T(8,128)(2,1)S(1)}, bf16[112,512]{1,0:T(8,128)(2,1)S(1)}, u32[]{:S(2)}, u32[]{:S(2)}) %collective-permute-start.1) | collective-permute-done | bytes 114720 | tf_op jit(solution)/shard_map/ppermute | solution.py:14
  240.3 10.1 %copy.30 = bf16[7168,512]{0,1:T(8,128)(2,1)} copy(bf16[7168,512]{1,0:T(8,128)(2,1)} %bitcast.6) | data formatting | bytes 14680064
  250.3 33.9 %while.24 = (s32[]{:T(128)}, f32[4,224]{1,0:T(4,128)S(1)}, s32[]{:T(128)}, bf16[7168,512]{0,1:T(8,128)(2,1)}, bf16[224,4,128]{2,0,1:T(8,128)(2,1)S(1)}, /*index=...) while((s32[]{:T(128)}, f32[4,224]{1,0:T(4,128)S(1)}, s32[]{:T(128)}, ...), condition=%wide.region_7.8_spmd.clone, body=%wide.region_5.7_spmd.clone.sunk | while | flops 118932200 | bytes 2052007 | solution.py:105
  250.3 1.1 constant_dynamic-slice_fusion.6
  252.7 1.1 constant_dynamic-slice_fusion.6
  255.2 1.1 constant_dynamic-slice_fusion.6
  257.6 1.1 constant_dynamic-slice_fusion.6
  260.0 1.1 constant_dynamic-slice_fusion.6
  262.4 1.1 constant_dynamic-slice_fusion.6
  264.8 1.1 constant_dynamic-slice_fusion.6
  267.3 1.1 constant_dynamic-slice_fusion.6
  269.7 1.1 constant_dynamic-slice_fusion.6
  272.1 1.1 constant_dynamic-slice_fusion.6
  274.5 1.1 constant_dynamic-slice_fusion.6
  277.0 1.1 constant_dynamic-slice_fusion.6
  279.4 1.1 constant_dynamic-slice_fusion.6
  281.8 1.1 constant_dynamic-slice_fusion.6
  284.3 61.6 %while.25 = (s32[]{:T(128)}, f32[4,224]{1,0:T(4,128)S(1)}, f32[4,224,128]{2,1,0:T(8,128)S(1)}, s32[]{:T(128)}, bf16[7168,512]{0,1:T(8,128)(2,1)}, /*index=5*/bf1...) while((s32[]{:T(128)}, f32[4,224]{1,0:T(4,128)S(1)}, ...), condition=%wide.region_10.11_spmd.clone, body=%wide.region_8.10_spmd.clone.sunk | while | flops 237404896 | bytes 7429571 | solution.py:114
  284.3 1.1 constant_dynamic-slice_fusion.7
  287.0 1.1 constant_dynamic-slice_fusion.8
  288.7 1.1 constant_dynamic-slice_fusion.7
  290.6 0.8 fusion.48
  291.4 1.1 constant_dynamic-slice_fusion.8
  293.1 1.1 constant_dynamic-slice_fusion.7
  295.0 0.8 fusion.48
  295.8 1.1 constant_dynamic-slice_fusion.8
  297.5 1.1 constant_dynamic-slice_fusion.7
  299.4 0.8 fusion.48
  300.2 1.1 constant_dynamic-slice_fusion.8
  301.9 1.1 constant_dynamic-slice_fusion.7
  303.8 0.8 fusion.48
  304.6 1.1 constant_dynamic-slice_fusion.8
  306.3 1.1 constant_dynamic-slice_fusion.7
  308.2 0.8 fusion.48
  309.0 1.1 constant_dynamic-slice_fusion.8
  310.7 1.1 constant_dynamic-slice_fusion.7
  313.4 1.1 constant_dynamic-slice_fusion.8
  315.1 1.1 constant_dynamic-slice_fusion.7
  317.8 1.1 constant_dynamic-slice_fusion.8
  319.5 1.1 constant_dynamic-slice_fusion.7
  322.2 1.1 constant_dynamic-slice_fusion.8
  323.9 1.1 constant_dynamic-slice_fusion.7
  326.6 1.1 constant_dynamic-slice_fusion.8
  328.3 1.1 constant_dynamic-slice_fusion.7
  331.0 1.1 constant_dynamic-slice_fusion.8
  332.7 1.1 constant_dynamic-slice_fusion.7
  335.4 1.1 constant_dynamic-slice_fusion.8
  337.1 1.1 constant_dynamic-slice_fusion.7
  339.8 1.1 constant_dynamic-slice_fusion.8
  341.5 1.1 constant_dynamic-slice_fusion.7
  344.2 1.1 constant_dynamic-slice_fusion.8
  345.9 0.9 fusion.8
  (186 shorter events, 48.6 us)
Async XLA Ops:
  7.3 4.1 %collective-permute-start = (bf16[2,1024]{1,0:T(2,128)(2,1)S(1)}, bf16[2,1024]{1,0:T(2,128)(2,1)S(1)}, u32[]{:S(2)}, u32[]{:S(2)}) collective-permute-start(bf16[2,1024]{1,0:T(2,128)(2,1)S(1)} %slice.24), channel_id=1, source_target_pairs={{0,4},{4,8},{8,12},{12,16},{16,20},{20,24},{24,28},{28,32},{32,36}... | collective-permute-start | bytes 12296 | tf_op jit(solution)/shard_map/ppermute | solution.py:14
  42.7 197.5 %all-to-all-start = ((bf16[64,112,512]{2,1,0:T(8,128)(2,1)}), bf16[64,112,512]{2,1,0:T(8,128)(2,1)}, u32[]{:S(2)}, u32[]{:S(2)}) async-start(bf16[64,112,512]{2,1,0:T(8,128)(2,1)} %stack.2), calls=%async_computation | async-start | bytes 14680064 | tf_op jit(solution)/shard_map/all_to_all | solution.py:92
  58.7 3.7 %copy-start = (s32[64]{0:T(128)S(1)}, s32[64]{0:T(128)}, u32[]{:S(2)}) copy-start(s32[64]{0:T(128)} %param.15) | copy-start | bytes 772
  58.7 225.5 %all-gather.2.cloned.1.call-start = ((), (), s32[]{:S(2)}) async-start(), calls=%async_computation.1 | async-start | bytes 7454720 | tf_op jit(solution)/shard_map/all_gather | solution.py:94
  66.4 173.7 %collective-permute-start.1 = (bf16[112,512]{1,0:T(8,128)(2,1)S(1)}, bf16[112,512]{1,0:T(8,128)(2,1)S(1)}, u32[]{:S(2)}, u32[]{:S(2)}) collective-permute-start(bf16[112,512]{1,0:T(8,128)(2,1)S(1)} %convolution_convert_fusion.1), channel_id=1, source_target_pairs={{4,0},{8,4},{12,8},{16,12},{20,16},{24,20},{28,24},{32,28},{36,32}... | collective-permute-start | bytes 344072 | tf_op jit(solution)/shard_map/ppermute | solution.py:14
Sparse Core Ops, SparseCore 0:
  62.5 119.0 all-gather.1
